TPU v7x, 256 devices: a whole 4x4x8 slice. The times are simulated.
256 devices in a mesh: ctx: 8 (over z_lo, y), exp: 32 (over z_hi, x, core).
Axes of the slice: x: 4, y: 4, z: 8 (z_hi: 4, z_lo: 2; z = z_hi * 2 + z_lo), core: 2. Of those that a mesh axis runs over, the one named last changes fastest.
Arguments:
- tokens: bfloat16 [32, 1024, 2048], P('exp', 'ctx'), may hold values from -6 to 6
- queries: bfloat16 [32, 1024, 1024], P('exp', 'ctx'), may hold values from -60 to 60
- keys: bfloat16 [32, 1024, 1024], P('exp', 'ctx'), may hold values from -4 to 4
- values: bfloat16 [32, 1024, 1024], P('exp', 'ctx'), may hold values from -12 to 12
- out_proj: bfloat16 [1024, 2048], replicated, may hold values from -0.1875 to 0.1875
- mod_scale: float32 [32, 2048], P('exp'), may hold values from -2.5 to 2.5
- mod_shift: float32 [32, 2048], P('exp'), may hold values from -2.5 to 2.5
- expert_ids: int32 [32, 1024, 2], P('exp', 'ctx'), may hold values from 0 to 63, all different within a row; in each aligned block of 128 rows (0 to 127, 128 to 255, ..., all dimensions but the last counted through in order) at most 6 rows name the same one
- gates: float32 [32, 1024, 2], P('exp', 'ctx'), may hold values from 0.2 to 1
- w_gate: bfloat16 [65536, 2048], P(('ctx', 'exp')), may hold values from -0.125 to 0.125
- w_up: bfloat16 [65536, 2048], P(('ctx', 'exp')), may hold values from -0.125 to 0.125
- w_down: bfloat16 [65536, 2048], P(('ctx', 'exp')), may hold values from -0.1875 to 0.1875
- out_grad: bfloat16 [32, 1024, 2048], P('exp', 'ctx'), may hold values from -0.1875 to 0.1875
Outputs:
- layer_out: bfloat16 [32, 1024, 2048], P('exp', 'ctx')
- grad_gate: bfloat16 [65536, 2048], P(('ctx', 'exp'))
- grad_up: bfloat16 [65536, 2048], P(('ctx', 'exp'))
- grad_down: bfloat16 [65536, 2048], P(('ctx', 'exp'))
Inputs may be any that keep to these rules, and one draw needn't show every extreme that they name: `expert_ids`: the two ids of a token differ. Among the 128 tokens of one device no expert is named more than 6 times, and in some device some expert exactly 6 times.
All inputs are finite; a program needn't handle non-finite values.
Results may differ from a plain program's by a relative error of at most 0.0075.
Values may be sent and summed in bfloat16 or wider, within the bound.
A program may use at most 128 MiB of HBM per device.

v0:
```python
import jax
import jax.numpy as jnp
from jax import lax
from jax.sharding import PartitionSpec as P

HEADS = 8
HD = 128
SHARDS = 4


def per_device(
    tokens,
    queries,
    keys,
    values,
    out_proj,
    mod_scale,
    mod_shift,
    expert_ids,
    gates,
    w_gate,
    w_up,
    w_down,
    out_grad,
):
    ctx_count = lax.axis_size("ctx")
    exp_count = lax.axis_size("exp")
    local_tokens = tokens.shape[1]
    model_width = tokens.shape[2]
    score_scale = HD ** (-0.5)
    query_rows = queries[0]
    key_rows = keys[0]
    value_rows = values[0]
    query_heads = query_rows.reshape(local_tokens, HEADS, HD)
    running_top = jnp.full((HEADS, local_tokens), -1e30, jnp.float32)
    key_piece = lax.all_gather(key_rows, "ctx", axis=0, tiled=True).reshape(-1, HEADS, HD)
    value_piece = lax.all_gather(value_rows, "ctx", axis=0, tiled=True).reshape(-1, HEADS, HD)
    scores = (
        jnp.einsum("qhd,khd->hqk", query_heads, key_piece, preferred_element_type=jnp.float32)
        * score_scale
    )
    new_top = jnp.maximum(running_top, jnp.max(scores, axis=-1))
    exponent = jnp.exp(scores - new_top[..., None])
    running_sum = jnp.sum(exponent, axis=-1)
    accum = jnp.einsum(
        "hqk,khd->hqd",
        exponent.astype(jnp.bfloat16),
        value_piece,
        preferred_element_type=jnp.float32,
    )
    attended = (
        jnp.transpose(accum / running_sum[..., None], (1, 0, 2))
        .reshape(local_tokens, HEADS * HD)
        .astype(jnp.bfloat16)
    )
    mixed = tokens[0].astype(jnp.float32) + jnp.dot(
        attended, out_proj, preferred_element_type=jnp.float32
    )
    mean_square = jnp.mean(mixed * mixed, axis=-1, keepdims=True)
    normed = (mixed * lax.rsqrt(mean_square + 1e-06) * (1.0 + mod_scale) + mod_shift).astype(
        jnp.bfloat16
    )
    expert_total = ctx_count * exp_count // SHARDS
    capacity = 3 * local_tokens // expert_total
    group_count = exp_count // SHARDS
    chosen = expert_ids[0].reshape(-1)
    one_hot = (chosen[:, None] == jnp.arange(expert_total, dtype=jnp.int32)[None, :]).astype(
        jnp.int32
    )
    before = jnp.cumsum(one_hot, axis=0) - one_hot
    slot_index = jnp.sum(one_hot * before, axis=1)
    position = chosen * capacity + slot_index
    chooser = (
        jnp.arange(expert_total * capacity, dtype=jnp.int32)[:, None] == position[None, :]
    ).astype(jnp.bfloat16)
    gate_flat = gates[0].reshape(-1)
    token_rows = jnp.repeat(normed, 2, axis=0)
    grad_rows = (
        gate_flat[:, None] * jnp.repeat(out_grad[0], 2, axis=0).astype(jnp.float32)
    ).astype(jnp.bfloat16)
    stacked = jnp.concatenate([token_rows, grad_rows], axis=1)
    placed = jnp.dot(chooser, stacked, preferred_element_type=jnp.float32).astype(jnp.bfloat16)
    slot_width = capacity * 2 * model_width
    plain_slots = placed.reshape(ctx_count, group_count, slot_width)
    middle = lax.all_to_all(plain_slots, "ctx", split_axis=0, concat_axis=0, tiled=True)
    shaped = middle.reshape(ctx_count, group_count, 1, slot_width)
    widened = jnp.broadcast_to(shaped, (ctx_count, group_count, SHARDS, slot_width))
    arrived = lax.all_to_all(
        widened.reshape(ctx_count, exp_count, slot_width),
        "exp",
        split_axis=1,
        concat_axis=1,
        tiled=True,
    )
    arrived = arrived.reshape(-1, 2 * model_width)
    expert_rows = arrived[:, :model_width]
    row_grads = arrived[:, model_width:]
    gate_pre = jnp.einsum("rd,fd->rf", expert_rows, w_gate, preferred_element_type=jnp.float32)
    up_pre = jnp.einsum("rd,fd->rf", expert_rows, w_up, preferred_element_type=jnp.float32)
    sigmoid_gate = jax.nn.sigmoid(gate_pre)
    activation = gate_pre * sigmoid_gate
    hidden = (activation * up_pre).astype(jnp.bfloat16)
    piece_out = jnp.einsum("rf,fd->rd", hidden, w_down, preferred_element_type=jnp.float32).astype(
        jnp.bfloat16
    )
    out_width = capacity * model_width
    piece_out = piece_out.reshape(ctx_count, exp_count, out_width)
    by_piece = lax.all_to_all(piece_out, "exp", split_axis=1, concat_axis=1, tiled=True)
    piece_sums = jnp.sum(
        by_piece.astype(jnp.float32).reshape(ctx_count, group_count, SHARDS, out_width), axis=2
    )
    expert_sums = lax.all_to_all(
        piece_sums.astype(jnp.bfloat16), "ctx", split_axis=0, concat_axis=0, tiled=True
    ).astype(piece_sums.dtype)
    expert_sums = expert_sums.reshape(expert_total * capacity, model_width)
    hidden_grad = jnp.einsum("rd,fd->rf", row_grads, w_down, preferred_element_type=jnp.float32)
    gate_cot = (
        hidden_grad * up_pre * sigmoid_gate * (1.0 + gate_pre * (1.0 - sigmoid_gate))
    ).astype(jnp.bfloat16)
    up_cot = (hidden_grad * activation).astype(jnp.bfloat16)
    grad_down = jnp.einsum(
        "rf,rd->fd", hidden, row_grads, preferred_element_type=jnp.float32
    ).astype(jnp.bfloat16)
    grad_gate = jnp.einsum(
        "rf,rd->fd", gate_cot, expert_rows, preferred_element_type=jnp.float32
    ).astype(jnp.bfloat16)
    grad_up = jnp.einsum(
        "rf,rd->fd", up_cot, expert_rows, preferred_element_type=jnp.float32
    ).astype(jnp.bfloat16)
    picked = jnp.take(expert_sums, position, axis=0)
    combined = jnp.sum((gate_flat[:, None] * picked).reshape(local_tokens, 2, model_width), axis=1)
    layer_out = (mixed + combined).astype(jnp.bfloat16)[None]
    return (layer_out, grad_gate, grad_up, grad_down)


def solution(mesh):
    placed = (
        P("exp", "ctx", None),
        P("exp", "ctx", None),
        P("exp", "ctx", None),
        P("exp", "ctx", None),
        P(),
        P("exp", None),
        P("exp", None),
        P("exp", "ctx", None),
        P("exp", "ctx", None),
        P(("ctx", "exp"), None),
        P(("ctx", "exp"), None),
        P(("ctx", "exp"), None),
        P("exp", "ctx", None),
    )
    return jax.shard_map(
        per_device,
        mesh=mesh,
        in_specs=placed,
        out_specs=(
            P("exp", "ctx", None),
            P(("ctx", "exp"), None),
            P(("ctx", "exp"), None),
            P(("ctx", "exp"), None),
        ),
        check_vma=False,
    )
```

profile of v0, /device:TPU:3, one launch (start us, length us, event | category | flops | bytes accessed | tf_op | source)
XLA Modules:
  0.0 742.8 jit_solution(3102636036667470510)
XLA Ops:
  22.2 34.2 %all-gather.5.cloned.1.call-done = bf16[1,1024,1024]{1,2,0:T(8,128)(2,1)} async-done(((bf16[1,128,1024]{1,2,0:T(8,128)(2,1)}), bf16[1,1024,1024]{1,2,0:T(8,128)(2,1)}) %all-gather.5.cloned.1.call-update) | async-done | bytes 2097168 | tf_op jit(solution)/shard_map/all_gather | solution.py:36
  61.7 40.5 %all-gather.7.cloned.1.call-done = bf16[1,1024,1024]{2,1,0:T(8,128)(2,1)} async-done(((bf16[1,128,1024]{2,1,0:T(8,128)(2,1)}), bf16[1,1024,1024]{2,1,0:T(8,128)(2,1)}) %all-gather.7.cloned.1.call-update) | async-done | bytes 2097168 | tf_op jit(solution)/shard_map/all_gather | solution.py:37
  111.6 4.2 convolution_convert_fusion.1
  115.7 6.3 reshape.143
  122.0 35.0 %all_to_all.20 = bf16[8,8,24576]{2,1,0:T(8,128)(2,1)S(1)} all-to-all(bf16[8,8,24576]{2,1,0:T(8,128)(2,1)} %reshape.143), channel_id=1, replica_groups=mesh['ctx'=8,'exp'=32] {'ctx'}, dimensions={0} | all-to-all | bytes 6291456 | tf_op jit(solution)/shard_map/all_to_all | solution.py:85
  160.4 8.0 %broadcast_in_dim.37 = bf16[8,8,4,24576]{3,0,2,1:T(8,128)(2,1)} broadcast(bf16[8,8,24576]{2,0,1:T(8,128)(2,1)} %copy.95), dimensions={0,1,3} | broadcast | bytes 15728640 | tf_op jit(solution)/shard_map/broadcast_in_dim | solution.py:87
  168.4 291.2 %all_to_all.21 = bf16[8,32,24576]{2,0,1:T(8,128)(2,1)S(1)} all-to-all(bf16[8,32,24576]{2,0,1:T(8,128)(2,1)} %bitcast.62), channel_id=1, replica_groups=mesh['ctx'=8,'exp'=32] {'exp'}, dimensions={1} | all-to-all | bytes 25165824 | tf_op jit(solution)/shard_map/all_to_all | solution.py:88
  459.6 19.8 %copy.96 = bf16[8,32,24576]{2,1,0:T(8,128)(2,1)} copy(bf16[8,32,24576]{2,0,1:T(8,128)(2,1)S(1)} %all_to_all.21) | data formatting | bytes 25165824 | tf_op jit(solution)/shard_map/all_to_all | solution.py:88
  479.5 20.7 %reshape.145 = bf16[1536,4096]{1,0:T(8,128)(2,1)} reshape(bf16[8,32,24576]{2,1,0:T(8,128)(2,1)} %copy.96) | data formatting | bytes 25165824 | tf_op jit(solution)/shard_map/reshape | solution.py:95
  500.2 4.9 fusion.10
  510.2 4.4 convolution_convert_fusion
  514.6 12.5 %reshape.146 = bf16[8,32,12288]{2,1,0:T(8,128)(2,1)} reshape(bf16[1536,2048]{1,0:T(8,128)(2,1)} %convolution_convert_fusion) | data formatting | bytes 12582912 | tf_op jit(solution)/shard_map/reshape | solution.py:107
  527.1 8.8 %copy.97 = bf16[8,32,12288]{2,0,1:T(8,128)(2,1)} copy(bf16[8,32,12288]{2,1,0:T(8,128)(2,1)} %reshape.146) | data formatting | bytes 12582912 | tf_op jit(solution)/shard_map/reshape | solution.py:107
  536.0 7.2 all-to-all-start.2
  544.0 141.3 %all-to-all-done.2 = bf16[8,32,12288]{2,0,1:T(8,128)(2,1)} async-done(((bf16[8,32,12288]{2,0,1:T(8,128)(2,1)}), bf16[8,32,12288]{2,0,1:T(8,128)(2,1)}, u32[]{:S(2)}, u32[]{:S(2)}) %all-to-all-start.2) | async-done | bytes 6291488 | tf_op jit(solution)/shard_map/all_to_all | solution.py:108
  685.3 3.7 bitcast_reduce_fusion
  691.0 4.3 all-to-all-start.3
  695.3 5.7 fusion.20
  701.1 4.9 fusion.2
  712.0 3.5 all-to-all-done.3
  715.6 4.4 reshape.154
  719.9 5.5 gather_fusion
  725.5 3.5 gather.7
  729.0 5.7 multiply_reduce_fusion.1
  (86 shorter events, 47.7 us)
Async XLA Ops:
  7.2 503.0 %copy-start = (bf16[256,2048]{1,0:T(8,128)(2,1)S(1)}, bf16[256,2048]{1,0:T(8,128)(2,1)}, u32[]{:S(2)}) copy-start(bf16[256,2048]{1,0:T(8,128)(2,1)} %param.24) | copy-start | bytes 3145732
  7.2 6.2 copy-start.4
  7.2 49.3 %all-gather.5.cloned.1.call-start = ((), (), s32[]{:S(2)}) async-start(), calls=%async_computation.4 | async-start | bytes 2359296 | tf_op jit(solution)/shard_map/all_gather | solution.py:36
  9.2 93.1 %all-gather.7.cloned.1.call-start = ((), (), s32[]{:S(2)}) async-start(), calls=%async_computation.5 | async-start | bytes 2359296 | tf_op jit(solution)/shard_map/all_gather | solution.py:37
  16.0 2.7 copy-start.9
  16.0 4.3 copy-start.8
  58.8 1.9 copy-start.1
  105.1 3.5 copy-start.3
  105.1 3.6 copy-start.5
  108.7 0.8 copy-start.7
  479.5 20.7 %copy-start.10 = (bf16[256,2048]{1,0:T(8,128)(2,1)S(1)}, bf16[256,2048]{1,0:T(8,128)(2,1)}, u32[]{:S(2)}) copy-start(bf16[256,2048]{1,0:T(8,128)(2,1)} %param.22) | copy-start | bytes 3145732
  500.2 6.4 copy-start.2
  500.2 6.6 copy-start.11
  506.8 3.4 copy-start.12
  536.0 7.4 copy-start.6
  536.0 149.3 %all-to-all-start.2 = ((bf16[8,32,12288]{2,0,1:T(8,128)(2,1)}), bf16[8,32,12288]{2,0,1:T(8,128)(2,1)}, u32[]{:S(2)}, u32[]{:S(2)}) async-start(bf16[8,32,12288]{2,0,1:T(8,128)(2,1)} %copy.97), calls=%async_computation.2 | async-start | bytes 12582912 | tf_op jit(solution)/shard_map/all_to_all | solution.py:108
  691.0 24.6 %all-to-all-start.3 = ((bf16[8,8,12288]{2,1,0:T(8,128)(2,1)}), bf16[8,8,12288]{2,1,0:T(8,128)(2,1)}, u32[]{:S(2)}, u32[]{:S(2)}) async-start(bf16[8,8,12288]{2,1,0:T(8,128)(2,1)} %copy.98), calls=%async_computation.3 | async-start | bytes 3145728 | tf_op jit(solution)/shard_map/all_to_all | solution.py:112
  695.3 10.6 %slice-start = ((s8[12582912]{0:T(1024)(128)(4,1)}), s8[4194304]{0:T(1024)(128)(4,1)S(1)}, s32[]{:S(2)}) async-start(s8[12582912]{0:T(1024)(128)(4,1)} %bitcast.63), calls=%async_computation.6 | async-start | bytes 8388608
  695.3 10.6 %slice-start.1 = ((s8[12582912]{0:T(1024)(128)(4,1)}), s8[4194304]{0:T(1024)(128)(4,1)S(1)}, s32[]{:S(2)}) async-start(s8[12582912]{0:T(1024)(128)(4,1)} %bitcast.63), calls=%async_computation.7 | async-start | bytes 8388608
  701.1 4.9 slice-start.2
  701.1 4.9 copy-start.13
  706.0 2.9 copy-start.14
Sparse Core Ops, SparseCore 0:
  10.3 46.1 all-gather.4
  58.3 43.9 all-gather.6
where the time goes:
time: 751 us; the launch traced here: 743 us
  blocking collectives  326 us (43%)
  waiting for transfers between devices  220 us (29%)
  local copies, waits for them, and re-layouts  115 us (15%)
  matrix products  40 us (5%)
  other arithmetic  14.9 us (2%)
  between operations  14.8 us (2%)
  starting transfers between devices  11.6 us (2%)
    all_to_all x1, blocking collectives, per_device(): lax.all_to_all(widened.reshape(ctx_count, exp_count, slot_width), 'exp',...  291 us
    all_to_all x1, waiting for transfers between devices, per_device(): lax.all_to_all(piece_out, 'exp', split_axis=1, concat_axis=1, tiled=True)  141 us
    all_gather x1, waiting for transfers between devices, per_device(): lax.all_gather(value_rows, 'ctx', axis=0, tiled=True).reshape(-1, HEADS, HD)  40.5 us
    all_to_all x1, blocking collectives, per_device(): lax.all_to_all(plain_slots, 'ctx', split_axis=0, concat_axis=0, tiled=True)  35 us
    all_gather x1, waiting for transfers between devices, per_device(): lax.all_gather(key_rows, 'ctx', axis=0, tiled=True).reshape(-1, HEADS, HD)  34.2 us
    reshape x2, local copies, waits for them, and re-layouts, per_device(): piece_out = piece_out.reshape(ctx_count, exp_count, out_width)  21.4 us
    reshape x1, local copies, waits for them, and re-layouts, per_device(): arrived = arrived.reshape(-1, 2 * model_width)  20.7 us
    all_to_all x1, local copies, waits for them, and re-layouts, per_device(): lax.all_to_all(widened.reshape(ctx_count, exp_count, slot_width), 'exp',...  19.8 us
  transfers between devices with their start and end apart: 4, of which 4 were waited for; matrix products, arithmetic and copies ran while one was open for 4% of the time, Pallas kernels for 0%

commit v1 on v0

--- a/solution.py
+++ b/solution.py
@@ -33,7 +33,10 @@
     value_rows = values[0]
     query_heads = query_rows.reshape(local_tokens, HEADS, HD)
     running_top = jnp.full((HEADS, local_tokens), -1e30, jnp.float32)
-    key_piece = lax.all_gather(key_rows, "ctx", axis=0, tiled=True).reshape(-1, HEADS, HD)
+    types_unite = lambda z_in, net_axis, axis_k: jnp.concatenate(
+        lax.all_to_all(jnp.stack(lax.axis_size(net_axis) * [z_in]), net_axis, 0, 0), axis=axis_k
+    )
+    key_piece = types_unite(key_rows, "ctx", 0).reshape(-1, HEADS, HD)
     value_piece = lax.all_gather(value_rows, "ctx", axis=0, tiled=True).reshape(-1, HEADS, HD)
     scores = (
         jnp.einsum("qhd,khd->hqk", query_heads, key_piece, preferred_element_type=jnp.float32)

time: 751 us -> 716 us (0.953)
  waiting for transfers between devices: 220 us -> 173 us
    all_gather x1 -> x0, waiting for transfers between devices: 34.2 us -> none  [per_device(): lax.all_gather(key_rows, 'ctx', axis=0, tiled=True).reshape(-1, HEADS, HD)]
    all_gather x1, waiting for transfers between devices: 40.5 us -> 13 us  [per_device(): lax.all_gather(value_rows, 'ctx', axis=0, tiled=True).reshape(-1, HEADS, HD)]
    all_to_all x0 -> x1, waiting for transfers between devices: none -> 15.7 us  [per_device(): lax.all_to_all(jnp.stack(lax.axis_size(net_axis) * [z_in]), net_axis, 0, 0)]
  transfers between devices with their start and end apart: 4 -> 4, of which waited for: 4 -> 4; matrix products, arithmetic and copies ran while one was open for 4% -> 5% of each run, Pallas kernels for 0% -> 0%
where the time goes in v1:
time: 716 us; the launch traced here: 706 us
  blocking collectives  329 us (46%)
  waiting for transfers between devices  173 us (24%)
  local copies, waits for them, and re-layouts  117 us (16%)
  matrix products  38.5 us (5%)
  starting transfers between devices  17.2 us (2%)
  other arithmetic  16.8 us (2%)
  between operations  14.8 us (2%)
    all_to_all x1, blocking collectives, per_device(): lax.all_to_all(widened.reshape(ctx_count, exp_count, slot_width), 'exp',...  289 us
    all_to_all x1, waiting for transfers between devices, per_device(): lax.all_to_all(piece_out, 'exp', split_axis=1, concat_axis=1, tiled=True)  140 us
    all_to_all x1, blocking collectives, per_device(): lax.all_to_all(plain_slots, 'ctx', split_axis=0, concat_axis=0, tiled=True)  39.6 us
    reshape x2, local copies, waits for them, and re-layouts, per_device(): piece_out = piece_out.reshape(ctx_count, exp_count, out_width)  21.4 us
    reshape x1, local copies, waits for them, and re-layouts, per_device(): arrived = arrived.reshape(-1, 2 * model_width)  20.7 us
    all_to_all x1, local copies, waits for them, and re-layouts, per_device(): lax.all_to_all(widened.reshape(ctx_count, exp_count, slot_width), 'exp',...  19.9 us
    all_to_all x1, waiting for transfers between devices, per_device(): lax.all_to_all(jnp.stack(lax.axis_size(net_axis) * [z_in]), net_axis, 0, 0)  15.7 us
  transfers between devices with their start and end apart: 4, of which 4 were waited for; matrix products, arithmetic and copies ran while one was open for 5% of the time, Pallas kernels for 0%

profile of v1, /device:TPU:3, one launch (start us, length us, event | category | flops | bytes accessed | tf_op | source)
XLA Modules:
  0.0 706.4 jit_solution(16591076374008990344)
XLA Ops:
  9.8 5.7 all-to-all-start
  31.5 15.7 %all-to-all-done = bf16[8,128,1024]{2,1,0:T(8,128)(2,1)S(1)} async-done(((bf16[8,128,1024]{2,1,0:T(8,128)(2,1)}), bf16[8,128,1024]{2,1,0:T(8,128)(2,1)S(1)}, u32[]{:S(2)}, u32[]{:S(2)}) %all-to-all-start) | async-done | bytes 2097184 | tf_op jit(solution)/shard_map/all_to_all | solution.py:37
  51.5 13.0 %all-gather.3.cloned.1.call-done = bf16[1,1024,1024]{2,1,0:T(8,128)(2,1)} async-done(((bf16[1,128,1024]{2,1,0:T(8,128)(2,1)}), bf16[1,1024,1024]{2,1,0:T(8,128)(2,1)}) %all-gather.3.cloned.1.call-update) | async-done | bytes 2097168 | tf_op jit(solution)/shard_map/all_gather | solution.py:40
  73.9 4.2 convolution_convert_fusion.1
  78.1 6.3 reshape.140
  84.3 39.6 %all_to_all.25 = bf16[8,8,24576]{2,1,0:T(8,128)(2,1)S(1)} all-to-all(bf16[8,8,24576]{2,1,0:T(8,128)(2,1)} %reshape.140), channel_id=1, replica_groups=mesh['ctx'=8,'exp'=32] {'ctx'}, dimensions={0} | all-to-all | bytes 6291456 | tf_op jit(solution)/shard_map/all_to_all | solution.py:88
  127.3 8.0 %broadcast_in_dim.37 = bf16[8,8,4,24576]{3,0,2,1:T(8,128)(2,1)} broadcast(bf16[8,8,24576]{2,0,1:T(8,128)(2,1)} %copy.89), dimensions={0,1,3} | broadcast | bytes 15728640 | tf_op jit(solution)/shard_map/broadcast_in_dim | solution.py:90
  135.3 289.1 %all_to_all.26 = bf16[8,32,24576]{2,0,1:T(8,128)(2,1)S(1)} all-to-all(bf16[8,32,24576]{2,0,1:T(8,128)(2,1)} %bitcast.64), channel_id=1, replica_groups=mesh['ctx'=8,'exp'=32] {'exp'}, dimensions={1} | all-to-all | bytes 25165824 | tf_op jit(solution)/shard_map/all_to_all | solution.py:91
  424.4 19.9 %copy.90 = bf16[8,32,24576]{2,1,0:T(8,128)(2,1)} copy(bf16[8,32,24576]{2,0,1:T(8,128)(2,1)S(1)} %all_to_all.26) | data formatting | bytes 25165824 | tf_op jit(solution)/shard_map/all_to_all | solution.py:91
  444.3 20.7 %reshape.142 = bf16[1536,4096]{1,0:T(8,128)(2,1)} reshape(bf16[8,32,24576]{2,1,0:T(8,128)(2,1)} %copy.90) | data formatting | bytes 25165824 | tf_op jit(solution)/shard_map/reshape | solution.py:98
  465.0 4.9 fusion.10
  475.0 4.4 convolution_convert_fusion
  479.4 12.5 %reshape.143 = bf16[8,32,12288]{2,1,0:T(8,128)(2,1)} reshape(bf16[1536,2048]{1,0:T(8,128)(2,1)} %convolution_convert_fusion) | data formatting | bytes 12582912 | tf_op jit(solution)/shard_map/reshape | solution.py:110
  491.9 8.8 %copy.91 = bf16[8,32,12288]{2,0,1:T(8,128)(2,1)} copy(bf16[8,32,12288]{2,1,0:T(8,128)(2,1)} %reshape.143) | data formatting | bytes 12582912 | tf_op jit(solution)/shard_map/reshape | solution.py:110
  500.8 7.2 %all-to-all-start.3 = ((bf16[8,32,12288]{2,0,1:T(8,128)(2,1)}), bf16[8,32,12288]{2,0,1:T(8,128)(2,1)}, u32[]{:S(2)}, u32[]{:S(2)}) async-start(bf16[8,32,12288]{2,0,1:T(8,128)(2,1)} %copy.91), calls=%async_computation.3 | async-start | bytes 12582912 | tf_op jit(solution)/shard_map/all_to_all | solution.py:111
  508.8 139.7 %all-to-all-done.3 = bf16[8,32,12288]{2,0,1:T(8,128)(2,1)} async-done(((bf16[8,32,12288]{2,0,1:T(8,128)(2,1)}), bf16[8,32,12288]{2,0,1:T(8,128)(2,1)}, u32[]{:S(2)}, u32[]{:S(2)}) %all-to-all-start.3) | async-done | bytes 6291488 | tf_op jit(solution)/shard_map/all_to_all | solution.py:111
  648.5 3.7 bitcast_reduce_fusion
  654.3 4.3 all-to-all-start.4
  658.6 5.7 fusion.20
  664.4 4.9 fusion.2
  675.3 3.9 all-to-all-done.4
  679.2 4.4 reshape.151
  683.6 5.5 gather_fusion
  692.6 5.7 multiply_reduce_fusion.1
  (84 shorter events, 53.9 us)
Async XLA Ops:
  7.2 467.8 %copy-start = (bf16[256,2048]{1,0:T(8,128)(2,1)S(1)}, bf16[256,2048]{1,0:T(8,128)(2,1)}, u32[]{:S(2)}) copy-start(bf16[256,2048]{1,0:T(8,128)(2,1)} %param.24) | copy-start | bytes 3145732
  9.8 6.4 copy-start.5
  9.8 37.3 %all-to-all-start = ((bf16[8,128,1024]{2,1,0:T(8,128)(2,1)}), bf16[8,128,1024]{2,1,0:T(8,128)(2,1)S(1)}, u32[]{:S(2)}, u32[]{:S(2)}) async-start(bf16[8,128,1024]{2,1,0:T(8,128)(2,1)} %stack.3), calls=%async_computation | async-start | bytes 4194304 | tf_op jit(solution)/shard_map/all_to_all | solution.py:37
  15.5 49.0 %all-gather.3.cloned.1.call-start = ((), (), s32[]{:S(2)}) async-start(), calls=%async_computation.5 | async-start | bytes 2359296 | tf_op jit(solution)/shard_map/all_gather | solution.py:40
  22.7 6.0 copy-start.7
  48.6 1.9 copy-start.1
  67.4 3.5 copy-start.3
  67.4 3.6 copy-start.4
  71.0 0.8 copy-start.6
  444.2 20.7 %copy-start.9 = (bf16[256,2048]{1,0:T(8,128)(2,1)S(1)}, bf16[256,2048]{1,0:T(8,128)(2,1)}, u32[]{:S(2)}) copy-start(bf16[256,2048]{1,0:T(8,128)(2,1)} %param.22) | copy-start | bytes 3145732
  465.0 6.4 copy-start.2
  465.0 6.6 copy-start.10
  471.6 3.4 copy-start.11
  500.8 7.9 %copy-start.8 = (f32[1,128,2]{1,2,0:T(2,128)S(1)}, f32[1,128,2]{1,2,0:T(2,128)}, u32[]{:S(2)}) copy-start(f32[1,128,2]{1,2,0:T(2,128)} %param.21) | copy-start | bytes 3076
  500.8 147.8 %all-to-all-start.3 = ((bf16[8,32,12288]{2,0,1:T(8,128)(2,1)}), bf16[8,32,12288]{2,0,1:T(8,128)(2,1)}, u32[]{:S(2)}, u32[]{:S(2)}) async-start(bf16[8,32,12288]{2,0,1:T(8,128)(2,1)} %copy.91), calls=%async_computation.3 | async-start | bytes 12582912 | tf_op jit(solution)/shard_map/all_to_all | solution.py:111
  654.3 24.9 %all-to-all-start.4 = ((bf16[8,8,12288]{2,1,0:T(8,128)(2,1)}), bf16[8,8,12288]{2,1,0:T(8,128)(2,1)}, u32[]{:S(2)}, u32[]{:S(2)}) async-start(bf16[8,8,12288]{2,1,0:T(8,128)(2,1)} %copy.92), calls=%async_computation.4 | async-start | bytes 3145728 | tf_op jit(solution)/shard_map/all_to_all | solution.py:115
  658.6 10.6 %slice-start = ((s8[12582912]{0:T(1024)(128)(4,1)}), s8[4194304]{0:T(1024)(128)(4,1)S(1)}, s32[]{:S(2)}) async-start(s8[12582912]{0:T(1024)(128)(4,1)} %bitcast.65), calls=%async_computation.6 | async-start | bytes 8388608
  658.6 10.6 %slice-start.1 = ((s8[12582912]{0:T(1024)(128)(4,1)}), s8[4194304]{0:T(1024)(128)(4,1)S(1)}, s32[]{:S(2)}) async-start(s8[12582912]{0:T(1024)(128)(4,1)} %bitcast.65), calls=%async_computation.7 | async-start | bytes 8388608
  664.3 4.9 slice-start.2
  664.3 4.9 copy-start.12
  669.3 2.9 copy-start.13
Sparse Core Ops, SparseCore 0:
  18.1 46.4 all-gather.2
